TPU v7x, 32 devices: a whole 2x2x4 slice. The times are simulated.
32 devices in a mesh: side: 2 (over x), grp: 2 (over core), pts: 8 (over z, y).
Axes of the slice: x: 2, y: 2, z: 4, core: 2. Of those that a mesh axis runs over, the one named last changes fastest.
Arguments:
- fields: bfloat16 [2, 4096, 2048], P('side', ('grp', 'pts')), may hold values from -6 to 6
- point_weight: float32 [2, 4096], P('side', ('grp', 'pts')), may hold values from 0.3 to 3
- start_modes: float32 [2, 32, 4096], P('side', None, ('grp', 'pts')), may hold values from -6 to 6
Outputs:
- modes: float32 [2, 32, 4096], P('side', None, ('grp', 'pts'))
All inputs are finite; a program needn't handle non-finite values.
Results may differ from a plain program's by a relative error of at most 0.0085.
Values may be sent and summed in bfloat16 or wider, within the bound.
No kernel may reach another device: no remote copies, remote signals or barrier semaphores. Data moves between devices by JAX's collectives and lax.ppermute only.
A program may use at most 64 MiB of HBM per device.

v0:
```python
import jax
import jax.numpy as jnp
from jax import lax
from jax.sharding import PartitionSpec as P

ITERS = 6


def from_partner(value, axis, apart):
    mask = 2**apart
    pairs = [(source, source ^ mask) for source in range(lax.axis_size(axis))]
    return lax.ppermute(value, axis, pairs)


def map_back(coeffs, anomaly):
    return lax.dot_general(
        coeffs, anomaly, (((1,), (1,)), ((), ())), preferred_element_type=jnp.float32
    )


def body(fields, point_weight, start_modes):
    local_field = fields[0]
    weight = point_weight[0]
    mode_rows = start_modes[0]
    samples = local_field.shape[1]
    total_points = local_field.shape[0] * lax.axis_size("grp") * lax.axis_size("pts")
    for iteration in range(ITERS):
        weighted = (mode_rows * weight[None, :]).astype(jnp.bfloat16)
        partial_value = jnp.dot(weighted, local_field, preferred_element_type=jnp.float32)
        coeffs = lax.psum(partial_value, ("grp", "pts")).astype(jnp.bfloat16)
        partner = from_partner(coeffs, "side", 0)
        mapped = map_back(partner, local_field)
        mapped = mapped * weight[None, :] / samples
        local_gram = lax.dot_general(
            mapped,
            mapped,
            (((1,), (1,)), ((), ())),
            precision=lax.Precision.HIGHEST,
            preferred_element_type=jnp.float32,
        )
        gram_sum = lax.psum(local_gram, ("grp", "pts")) / total_points
        factor = jnp.linalg.cholesky(gram_sum)
        mode_rows = lax.linalg.triangular_solve(factor, mapped, left_side=True, lower=True)
    return mode_rows[None]


def solution(mesh):
    placed = (
        P("side", ("grp", "pts"), None),
        P("side", ("grp", "pts")),
        P("side", None, ("grp", "pts")),
    )
    return jax.shard_map(
        body, mesh=mesh, in_specs=placed, out_specs=P("side", None, ("grp", "pts")), check_vma=False
    )
```

profile of v0, /device:TPU:1, one launch (start us, length us, event | category | flops | bytes accessed | tf_op | source)
XLA Modules:
  0.0 806.0 jit_solution(8234775146145503029)
XLA Ops:
  0.0 1.2 copy-done
  1.2 1.0 fusion.27
  2.3 65.6 %all-reduce.6 = bf16[32,2048]{1,0:T(8,128)(2,1)S(1)} all-reduce(f32[32,2048]{1,0:T(8,128)S(1)} %fusion.27), channel_id=1, replica_groups=mesh['side'=2,'grp'=2,'pts'=8] {'grp','pts'}, use_global_device_ids=true, to_apply=%region_0.0 | all-reduce | flops 65536 | bytes 393216 | tf_op jit(solution)/shard_map/psum | solution.py:30
  67.9 1.3 collective-permute-start
  69.2 3.7 collective-permute-done
  72.9 0.4 fusion.5
  73.5 58.2 %psum.85 = f32[32,32]{0,1:T(8,128)S(1)} all-reduce(f32[32,32]{0,1:T(8,128)S(1)} %fusion.60), channel_id=1, replica_groups=mesh['side'=2,'grp'=2,'pts'=8] {'grp','pts'}, use_global_device_ids=true, to_apply=%region_1.0 | all-reduce | flops 1024 | bytes 8192 | tf_op jit(solution)/shard_map/psum | solution.py:41
  131.8 2.9 cholesky.104
  134.7 0.6 compare_reduce_fusion.5
  135.4 0.7 fusion.29
  136.0 2.4 custom-call.10
  138.7 0.3 fusion.24
  139.0 60.5 %all-reduce.7 = bf16[32,2048]{1,0:T(8,128)(2,1)S(1)} all-reduce(f32[32,2048]{1,0:T(8,128)S(1)} %fusion.24), channel_id=1, replica_groups=mesh['side'=2,'grp'=2,'pts'=8] {'grp','pts'}, use_global_device_ids=true, to_apply=%region_4.7 | all-reduce | flops 65536 | bytes 393216 | tf_op jit(solution)/shard_map/psum | solution.py:30
  199.5 1.0 collective-permute-start.1
  200.5 3.9 collective-permute-done.1
  204.4 0.4 fusion.4
  205.0 60.4 %psum.87 = f32[32,32]{0,1:T(8,128)S(1)} all-reduce(f32[32,32]{0,1:T(8,128)S(1)} %fusion.61), channel_id=1, replica_groups=mesh['side'=2,'grp'=2,'pts'=8] {'grp','pts'}, use_global_device_ids=true, to_apply=%region_5.8 | all-reduce | flops 1024 | bytes 8192 | tf_op jit(solution)/shard_map/psum | solution.py:41
  265.5 2.9 cholesky.115
  268.4 0.6 compare_reduce_fusion.4
  269.1 0.7 fusion.30
  269.7 2.4 custom-call.11
  272.4 0.3 fusion.21
  272.7 60.3 %all-reduce.8 = bf16[32,2048]{1,0:T(8,128)(2,1)S(1)} all-reduce(f32[32,2048]{1,0:T(8,128)S(1)} %fusion.21), channel_id=1, replica_groups=mesh['side'=2,'grp'=2,'pts'=8] {'grp','pts'}, use_global_device_ids=true, to_apply=%region_6.9 | all-reduce | flops 65536 | bytes 393216 | tf_op jit(solution)/shard_map/psum | solution.py:30
  333.0 1.3 collective-permute-start.2
  334.3 3.4 collective-permute-done.2
  337.7 0.4 fusion.3
  338.3 60.6 %psum.89 = f32[32,32]{0,1:T(8,128)S(1)} all-reduce(f32[32,32]{0,1:T(8,128)S(1)} %fusion.62), channel_id=1, replica_groups=mesh['side'=2,'grp'=2,'pts'=8] {'grp','pts'}, use_global_device_ids=true, to_apply=%region_7.10 | all-reduce | flops 1024 | bytes 8192 | tf_op jit(solution)/shard_map/psum | solution.py:41
  399.0 2.9 cholesky.126
  401.9 0.6 compare_reduce_fusion.3
  402.6 0.7 fusion.31
  403.2 2.4 custom-call.12
  405.9 0.3 fusion.18
  406.2 59.9 %all-reduce.9 = bf16[32,2048]{1,0:T(8,128)(2,1)S(1)} all-reduce(f32[32,2048]{1,0:T(8,128)S(1)} %fusion.18), channel_id=1, replica_groups=mesh['side'=2,'grp'=2,'pts'=8] {'grp','pts'}, use_global_device_ids=true, to_apply=%region_8.11 | all-reduce | flops 65536 | bytes 393216 | tf_op jit(solution)/shard_map/psum | solution.py:30
  466.1 1.2 collective-permute-start.3
  467.3 2.7 collective-permute-done.3
  469.9 0.4 fusion.2
  470.5 61.5 %psum.91 = f32[32,32]{0,1:T(8,128)S(1)} all-reduce(f32[32,32]{0,1:T(8,128)S(1)} %fusion.63), channel_id=1, replica_groups=mesh['side'=2,'grp'=2,'pts'=8] {'grp','pts'}, use_global_device_ids=true, to_apply=%region_9.12 | all-reduce | flops 1024 | bytes 8192 | tf_op jit(solution)/shard_map/psum | solution.py:41
  532.1 2.9 cholesky.137
  535.1 0.6 compare_reduce_fusion.2
  535.7 0.7 fusion.32
  536.4 2.4 custom-call.13
  538.8 0.2 fusion.9
  539.1 0.3 fusion.15
  539.4 60.2 %all-reduce.10 = bf16[32,2048]{1,0:T(8,128)(2,1)S(1)} all-reduce(f32[32,2048]{1,0:T(8,128)S(1)} %fusion.15), channel_id=1, replica_groups=mesh['side'=2,'grp'=2,'pts'=8] {'grp','pts'}, use_global_device_ids=true, to_apply=%region_10.13 | all-reduce | flops 65536 | bytes 393216 | tf_op jit(solution)/shard_map/psum | solution.py:30
  599.5 1.2 collective-permute-start.4
  600.7 2.7 collective-permute-done.4
  603.4 0.4 fusion.1
  604.0 61.3 %psum.93 = f32[32,32]{0,1:T(8,128)S(1)} all-reduce(f32[32,32]{0,1:T(8,128)S(1)} %fusion.64), channel_id=1, replica_groups=mesh['side'=2,'grp'=2,'pts'=8] {'grp','pts'}, use_global_device_ids=true, to_apply=%region_11.14 | all-reduce | flops 1024 | bytes 8192 | tf_op jit(solution)/shard_map/psum | solution.py:41
  665.4 2.9 cholesky.148
  668.4 0.6 compare_reduce_fusion.1
  669.0 0.7 fusion.33
  669.7 2.4 custom-call.14
  672.1 0.2 fusion.10
  672.4 0.3 fusion.12
  672.7 59.9 %all-reduce.11 = bf16[32,2048]{1,0:T(8,128)(2,1)S(1)} all-reduce(f32[32,2048]{1,0:T(8,128)S(1)} %fusion.12), channel_id=1, replica_groups=mesh['side'=2,'grp'=2,'pts'=8] {'grp','pts'}, use_global_device_ids=true, to_apply=%region_12.15 | all-reduce | flops 65536 | bytes 393216 | tf_op jit(solution)/shard_map/psum | solution.py:30
  732.6 1.2 collective-permute-start.5
  733.8 2.7 collective-permute-done.5
  736.5 0.4 fusion
  737.1 61.2 %psum.95 = f32[32,32]{0,1:T(8,128)S(1)} all-reduce(f32[32,32]{0,1:T(8,128)S(1)} %fusion.65), channel_id=1, replica_groups=mesh['side'=2,'grp'=2,'pts'=8] {'grp','pts'}, use_global_device_ids=true, to_apply=%region_13.16 | all-reduce | flops 1024 | bytes 8192 | tf_op jit(solution)/shard_map/psum | solution.py:41
  798.4 2.9 cholesky.159
  801.4 0.6 compare_reduce_fusion
  802.0 0.7 fusion.34
  802.7 2.4 custom-call.15
  805.1 0.9 convolution_bitcast_fusion
  (36 shorter events, 2.4 us)
Async XLA Ops:
  0.0 1.2 copy-start
  0.0 1.2 copy-start.1
  67.9 5.0 collective-permute-start
  199.5 4.8 collective-permute-start.1
  333.0 4.7 collective-permute-start.2
  466.1 3.9 collective-permute-start.3
  599.5 3.9 collective-permute-start.4
  732.6 3.9 collective-permute-start.5
where the time goes:
time: 806 us
  blocking collectives  730 us (91%)
  other arithmetic  40.2 us (5%)
  waiting for transfers between devices  19 us (2%)
    psum x6, blocking collectives, body(): coeffs = lax.psum(partial_value, ('grp', 'pts')).astype(jnp.bfloat16)  366 us
    psum x6, blocking collectives, body(): gram_sum = lax.psum(local_gram, ('grp', 'pts')) / total_points  363 us
    another operation x18, other arithmetic, body(): factor = jnp.linalg.cholesky(gram_sum)  21.6 us
    ppermute x6, waiting for transfers between devices, from_partner(): return lax.ppermute(value, axis, pairs)  19 us
    another operation x12, other arithmetic, body(): lax.linalg.triangular_solve(factor, mapped, left_side=True, lower=True)  18.5 us
  transfers between devices with their start and end apart: 6, of which 6 were waited for; matrix products, arithmetic and copies ran while one was open for 0% of the time, Pallas kernels for 0%

commit v1 on v0

--- a/solution.py
+++ b/solution.py
@@ -27,7 +27,7 @@
     for iteration in range(ITERS):
         weighted = (mode_rows * weight[None, :]).astype(jnp.bfloat16)
         partial_value = jnp.dot(weighted, local_field, preferred_element_type=jnp.float32)
-        coeffs = lax.psum(partial_value, ("grp", "pts")).astype(jnp.bfloat16)
+        coeffs = jnp.sum(lax.all_gather(partial_value, ("grp", "pts")), axis=0).astype(jnp.bfloat16)
         partner = from_partner(coeffs, "side", 0)
         mapped = map_back(partner, local_field)
         mapped = mapped * weight[None, :] / samples

time: 806 us -> 766 us (0.950)
  blocking collectives: 730 us -> 362 us
  waiting for transfers between devices: 19 us -> 313 us
  other arithmetic: 40.2 us -> 54.8 us
  between operations: 0.26 us -> 13.7 us
    psum x6 -> x0, blocking collectives: 366 us -> none  [body(): coeffs = lax.psum(partial_value, ('grp', 'pts')).astype(jnp.bfloat16)]
    all_gather x0 -> x6, waiting for transfers between devices: none -> 291 us  [body(): lax.all_gather(partial_value, ('grp', 'pts'))]
    reduce_sum x0 -> x6, other arithmetic: none -> 14.6 us  [body(): jnp.sum(lax.all_gather(partial_value, ('grp', 'pts')), axis=0)]
  transfers between devices with their start and end apart: 6 -> 12, of which waited for: 6 -> 12; matrix products, arithmetic and copies ran while one was open for 0% -> 0% of each run, Pallas kernels for 0% -> 0%
where the time goes in v1:
time: 766 us; the launch traced here: 765 us
  blocking collectives  362 us (47%)
  waiting for transfers between devices  313 us (41%)
  other arithmetic  54.8 us (7%)
  between operations  13.7 us (2%)
  matrix products  12.2 us (2%)
  starting transfers between devices  7.73 us (1%)
    psum x6, blocking collectives, body(): gram_sum = lax.psum(local_gram, ('grp', 'pts')) / total_points  362 us
    all_gather x6, waiting for transfers between devices, body(): lax.all_gather(partial_value, ('grp', 'pts'))  291 us
    another operation x18, other arithmetic, body(): factor = jnp.linalg.cholesky(gram_sum)  21.6 us
    ppermute x6, waiting for transfers between devices, from_partner(): return lax.ppermute(value, axis, pairs)  21.6 us
    another operation x12, other arithmetic, body(): lax.linalg.triangular_solve(factor, mapped, left_side=True, lower=True)  18.5 us
  transfers between devices with their start and end apart: 12, of which 12 were waited for; matrix products, arithmetic and copies ran while one was open for 0% of the time, Pallas kernels for 0%

profile of v1, /device:TPU:1, one launch (start us, length us, event | category | flops | bytes accessed | tf_op | source)
XLA Modules:
  0.0 765.0 jit_solution(17112575137110300144)
XLA Ops:
  6.5 1.2 copy-done
  7.8 1.7 fusion.27
  9.6 52.9 %all-gather.13.cloned.1.call-done = f32[512,2048]{1,0:T(8,128)} async-done(((f32[32,2048]{1,0:T(8,128)}), f32[512,2048]{1,0:T(8,128)}) %all-gather.13.cloned.1.call-update) | async-done | bytes 4194320 | tf_op jit(solution)/shard_map/all_gather | solution.py:30
  62.5 2.4 reduce_sum.54
  65.0 1.3 collective-permute-start
  66.2 3.6 collective-permute-done
  69.8 0.4 fusion.5
  70.4 60.4 %psum.42 = f32[32,32]{0,1:T(8,128)S(1)} all-reduce(f32[32,32]{0,1:T(8,128)S(1)} %fusion.60), channel_id=1, replica_groups=mesh['side'=2,'grp'=2,'pts'=8] {'grp','pts'}, use_global_device_ids=true, to_apply=%region_1.0 | all-reduce | flops 1024 | bytes 8192 | tf_op jit(solution)/shard_map/psum | solution.py:41
  130.9 2.9 cholesky.104
  133.8 0.6 compare_reduce_fusion.5
  134.5 0.7 fusion.29
  135.1 2.4 custom-call.10
  137.8 1.0 fusion.24
  138.9 47.6 %all-gather.15.cloned.1.call-done = f32[512,2048]{1,0:T(8,128)} async-done(((f32[32,2048]{1,0:T(8,128)}), f32[512,2048]{1,0:T(8,128)}) %all-gather.15.cloned.1.call-update) | async-done | bytes 4194320 | tf_op jit(solution)/shard_map/all_gather | solution.py:30
  186.5 2.4 reduce_sum.55
  188.9 1.3 collective-permute-start.1
  190.1 3.6 collective-permute-done.1
  194.3 60.4 %psum.43 = f32[32,32]{0,1:T(8,128)S(1)} all-reduce(f32[32,32]{0,1:T(8,128)S(1)} %fusion.61), channel_id=1, replica_groups=mesh['side'=2,'grp'=2,'pts'=8] {'grp','pts'}, use_global_device_ids=true, to_apply=%region_5.8 | all-reduce | flops 1024 | bytes 8192 | tf_op jit(solution)/shard_map/psum | solution.py:41
  254.8 2.9 cholesky.115
  257.8 0.6 compare_reduce_fusion.4
  258.4 0.7 fusion.30
  259.1 2.4 custom-call.11
  261.8 1.0 fusion.21
  262.8 47.6 %all-gather.17.cloned.1.call-done = f32[512,2048]{1,0:T(8,128)} async-done(((f32[32,2048]{1,0:T(8,128)}), f32[512,2048]{1,0:T(8,128)}) %all-gather.17.cloned.1.call-update) | async-done | bytes 4194320 | tf_op jit(solution)/shard_map/all_gather | solution.py:30
  310.4 2.4 reduce_sum.56
  312.8 1.3 collective-permute-start.2
  314.1 3.6 collective-permute-done.2
  318.3 60.4 %psum.44 = f32[32,32]{0,1:T(8,128)S(1)} all-reduce(f32[32,32]{0,1:T(8,128)S(1)} %fusion.62), channel_id=1, replica_groups=mesh['side'=2,'grp'=2,'pts'=8] {'grp','pts'}, use_global_device_ids=true, to_apply=%region_7.10 | all-reduce | flops 1024 | bytes 8192 | tf_op jit(solution)/shard_map/psum | solution.py:41
  378.7 2.9 cholesky.126
  381.7 0.6 compare_reduce_fusion.3
  382.3 0.7 fusion.31
  383.0 2.4 custom-call.12
  385.7 1.0 fusion.18
  386.7 47.6 %all-gather.19.cloned.1.call-done = f32[512,2048]{1,0:T(8,128)} async-done(((f32[32,2048]{1,0:T(8,128)}), f32[512,2048]{1,0:T(8,128)}) %all-gather.19.cloned.1.call-update) | async-done | bytes 4194320 | tf_op jit(solution)/shard_map/all_gather | solution.py:30
  434.3 2.4 reduce_sum.57
  436.8 1.3 collective-permute-start.3
  438.0 3.6 collective-permute-done.3
  441.6 0.4 fusion.2
  442.2 60.4 %psum.45 = f32[32,32]{0,1:T(8,128)S(1)} all-reduce(f32[32,32]{0,1:T(8,128)S(1)} %fusion.63), channel_id=1, replica_groups=mesh['side'=2,'grp'=2,'pts'=8] {'grp','pts'}, use_global_device_ids=true, to_apply=%region_9.12 | all-reduce | flops 1024 | bytes 8192 | tf_op jit(solution)/shard_map/psum | solution.py:41
  502.7 2.9 cholesky.137
  505.6 0.6 compare_reduce_fusion.2
  506.3 0.7 fusion.32
  506.9 2.4 custom-call.13
  509.6 1.0 fusion.15
  510.7 47.6 %all-gather.21.cloned.1.call-done = f32[512,2048]{1,0:T(8,128)} async-done(((f32[32,2048]{1,0:T(8,128)}), f32[512,2048]{1,0:T(8,128)}) %all-gather.21.cloned.1.call-update) | async-done | bytes 4194320 | tf_op jit(solution)/shard_map/all_gather | solution.py:30
  558.3 2.4 reduce_sum.58
  560.7 1.3 collective-permute-start.4
  562.0 3.6 collective-permute-done.4
  566.2 60.4 %psum.46 = f32[32,32]{0,1:T(8,128)S(1)} all-reduce(f32[32,32]{0,1:T(8,128)S(1)} %fusion.64), channel_id=1, replica_groups=mesh['side'=2,'grp'=2,'pts'=8] {'grp','pts'}, use_global_device_ids=true, to_apply=%region_11.14 | all-reduce | flops 1024 | bytes 8192 | tf_op jit(solution)/shard_map/psum | solution.py:41
  626.6 2.9 cholesky.148
  629.6 0.6 compare_reduce_fusion.1
  630.2 0.7 fusion.33
  630.9 2.4 custom-call.14
  633.6 1.0 fusion.12
  634.6 47.6 %all-gather.23.cloned.1.call-done = f32[512,2048]{1,0:T(8,128)} async-done(((f32[32,2048]{1,0:T(8,128)}), f32[512,2048]{1,0:T(8,128)}) %all-gather.23.cloned.1.call-update) | async-done | bytes 4194320 | tf_op jit(solution)/shard_map/all_gather | solution.py:30
  682.2 2.4 reduce_sum.59
  684.6 1.3 collective-permute-start.5
  685.9 3.6 collective-permute-done.5
  690.1 60.4 %psum.47 = f32[32,32]{0,1:T(8,128)S(1)} all-reduce(f32[32,32]{0,1:T(8,128)S(1)} %fusion.65), channel_id=1, replica_groups=mesh['side'=2,'grp'=2,'pts'=8] {'grp','pts'}, use_global_device_ids=true, to_apply=%region_13.16 | all-reduce | flops 1024 | bytes 8192 | tf_op jit(solution)/shard_map/psum | solution.py:41
  750.6 2.9 cholesky.159
  753.5 0.6 compare_reduce_fusion
  754.2 0.7 fusion.34
  754.8 2.4 custom-call.15
  757.3 0.9 convolution_bitcast_fusion
  (54 shorter events, 4.9 us)
Async XLA Ops:
  6.5 1.2 copy-start
  6.5 63.3 %copy-start.1 = (f32[1,256]{1,0:T(1,128)S(1)}, f32[1,256]{1,0:T(1,128)}, u32[]{:S(2)}) copy-start(f32[1,256]{1,0:T(1,128)} %param.7) | copy-start | bytes 3076
  6.5 56.0 %all-gather.13.cloned.1.call-start = ((), (), s32[]{:S(2)}) async-start(), calls=%async_computation | async-start | bytes 4456448 | tf_op jit(solution)/shard_map/all_gather | solution.py:30
  9.5 176.9 %all-gather.15.cloned.1.call-start = ((), (), s32[]{:S(2)}) async-start(), calls=%async_computation.1 | async-start | bytes 4456448 | tf_op jit(solution)/shard_map/all_gather | solution.py:30
  65.0 4.8 collective-permute-start
  138.8 171.6 %all-gather.17.cloned.1.call-start = ((), (), s32[]{:S(2)}) async-start(), calls=%async_computation.2 | async-start | bytes 4456448 | tf_op jit(solution)/shard_map/all_gather | solution.py:30
  188.9 4.8 collective-permute-start.1
  262.8 171.6 %all-gather.19.cloned.1.call-start = ((), (), s32[]{:S(2)}) async-start(), calls=%async_computation.3 | async-start | bytes 4456448 | tf_op jit(solution)/shard_map/all_gather | solution.py:30
  312.8 4.8 collective-permute-start.2
  386.7 171.6 %all-gather.21.cloned.1.call-start = ((), (), s32[]{:S(2)}) async-start(), calls=%async_computation.4 | async-start | bytes 4456448 | tf_op jit(solution)/shard_map/all_gather | solution.py:30
  436.8 4.8 collective-permute-start.3
  510.6 171.6 %all-gather.23.cloned.1.call-start = ((), (), s32[]{:S(2)}) async-start(), calls=%async_computation.5 | async-start | bytes 4456448 | tf_op jit(solution)/shard_map/all_gather | solution.py:30
  560.7 4.8 collective-permute-start.4
  684.6 4.8 collective-permute-start.5
Sparse Core Ops, SparseCore 0:
  9.6 52.8 all-gather.12
  138.9 47.4 all-gather.14
  262.9 47.4 all-gather.16
  386.8 47.4 all-gather.18
  510.8 47.4 all-gather.20
  634.7 47.4 all-gather.22
